TPU v7x, 32 devices: a whole 2x2x4 slice. The times are simulated.
32 devices in a mesh: dp: 8 (over y, x, core), tensor: 4 (over z).
Axes of the slice: x: 2, y: 2, z: 4, core: 2. Of those that a mesh axis runs over, the one named last changes fastest.
Arguments:
- send_order: int32 [32, 32], P(('dp', 'tensor')), may hold values from 0 to 31, each once within a row
- master: float32 [32, 32, 2048], P(('dp', 'tensor')), may hold values from -6 to 6
- first_code: bfloat16 [32, 32, 2048], P(('dp', 'tensor')), may hold values from -1 to 1
- first_scale: float32 [32, 32], P(('dp', 'tensor')), may hold values from 0.1 to 2
- second_code: bfloat16 [32, 32, 2048], P(('dp', 'tensor')), may hold values from 0.049804688 to 1
- second_scale: float32 [32, 32], P(('dp', 'tensor')), may hold values from 0.5 to 20
- grads: bfloat16 [8, 4, 8, 32, 2048], P('dp', 'tensor'), may hold values from -6 to 6
Outputs:
- new_master: float32 [32, 32, 2048], P(('dp', 'tensor'))
- new_first_code: bfloat16 [32, 32, 2048], P(('dp', 'tensor'))
- new_first_scale: float32 [32, 32], P(('dp', 'tensor'))
- new_second_code: bfloat16 [32, 32, 2048], P(('dp', 'tensor'))
- new_second_scale: float32 [32, 32], P(('dp', 'tensor'))
- weights: bfloat16 [4, 8, 32, 2048], P('tensor')
Inputs may be any that keep to these rules, and one draw needn't show every extreme that they name: `send_order`: each row is an ordering of the slots 0 to 31, each once.
All inputs are finite; a program needn't handle non-finite values. Where the computation divides by a largest or mean magnitude, that divisor is 1e-20 or more.
Results may differ from a plain program's by a relative error of at most 0.001.
Values may be sent and summed in bfloat16 or wider, within the bound.
A program may use at most 128 MiB of HBM per device.

v0:
```python
import jax
import jax.numpy as jnp
from jax import lax
from jax.sharding import PartitionSpec as P

STEP = 10


def on_device(send_order, master, first_code, first_scale, second_code, second_scale, grads):
    count_dp = lax.axis_size("dp")
    count_tensor = lax.axis_size("tensor")
    devices_all = count_dp * count_tensor
    slots = master.shape[1]
    width = master.shape[2]
    per_peer = slots // devices_all
    order_row = send_order[0]
    moved = (
        master[0][order_row],
        first_code[0][order_row],
        first_scale[0][order_row],
        second_code[0][order_row],
        second_scale[0][order_row],
    )
    shaped = tuple((item.reshape((devices_all, per_peer) + item.shape[1:]) for item in moved))
    arrived = (
        lax.all_to_all(shaped[0], ("dp", "tensor"), split_axis=0, concat_axis=0, tiled=True),
        lax.all_to_all(
            shaped[1].astype(jnp.float32), ("dp", "tensor"), split_axis=0, concat_axis=0, tiled=True
        ).astype(jnp.bfloat16),
        lax.all_to_all(shaped[2], ("dp", "tensor"), split_axis=0, concat_axis=0, tiled=True),
        lax.all_to_all(
            shaped[3].astype(jnp.float32), ("dp", "tensor"), split_axis=0, concat_axis=0, tiled=True
        ).astype(jnp.bfloat16),
        lax.all_to_all(shaped[4], ("dp", "tensor"), split_axis=0, concat_axis=0, tiled=True),
    )
    master_new = arrived[0].reshape(slots, width)
    code_one = arrived[1].reshape(slots, width)
    scale_one = arrived[2].reshape(slots)
    code_two = arrived[3].reshape(slots, width)
    scale_two = arrived[4].reshape(slots)
    summed = lax.psum_scatter(grads.astype(jnp.float32), "dp", scatter_dimension=2, tiled=True)
    grad = summed.reshape(slots, width)
    first = code_one.astype(jnp.float32) * scale_one[:, None]
    second = code_two.astype(jnp.float32) * scale_two[:, None]
    moment_one = 0.9 * first + 0.1 * grad
    moment_two = 0.95 * second + 0.05 * grad * grad
    corr_one = 1.0 - 0.9**STEP
    corr_two = 1.0 - 0.95**STEP
    update = moment_one / corr_one / (jnp.sqrt(moment_two / corr_two) + 1e-08) + 0.1 * master_new
    new_master = master_new - 0.01 * update
    new_scale_one = jnp.max(jnp.abs(moment_one), axis=1) + 1e-06
    new_code_one = (moment_one / new_scale_one[:, None]).astype(jnp.bfloat16)
    new_scale_two = jnp.max(jnp.abs(moment_two), axis=1) + 1e-06
    new_code_two = (moment_two / new_scale_two[:, None]).astype(jnp.bfloat16)
    local_weights = new_master.astype(jnp.bfloat16).reshape(1, 1, slots, width)
    weights = lax.all_gather(local_weights, "dp", axis=1, tiled=True)
    return (
        new_master.reshape(1, slots, width),
        new_code_one.reshape(1, slots, width),
        new_scale_one.reshape(1, slots),
        new_code_two.reshape(1, slots, width),
        new_scale_two.reshape(1, slots),
        weights,
    )


def solution(mesh):
    placed = (
        P(("dp", "tensor"), None),
        P(("dp", "tensor"), None, None),
        P(("dp", "tensor"), None, None),
        P(("dp", "tensor"), None),
        P(("dp", "tensor"), None, None),
        P(("dp", "tensor"), None),
        P("dp", "tensor", None, None, None),
    )
    return jax.shard_map(
        on_device,
        mesh=mesh,
        in_specs=placed,
        out_specs=(
            P(("dp", "tensor"), None, None),
            P(("dp", "tensor"), None, None),
            P(("dp", "tensor"), None),
            P(("dp", "tensor"), None, None),
            P(("dp", "tensor"), None),
            P("tensor", None, None, None),
        ),
        check_vma=False,
    )
```

profile of v0, /device:TPU:0, one launch (start us, length us, event | category | flops | bytes accessed | tf_op | source)
XLA Modules:
  0.0 104.7 jit_solution(7902596441690301470)
XLA Ops:
  7.2 2.9 %bitcast_convert_fusion = f32[1,1,8,32,2048]{4,3,1,0,2:T(8,128)} fusion(bf16[1,1,8,32,2048]{4,3,2,1,0:T(8,128)(2,1)} %param.13), kind=kLoop, calls=%fused_computation.5 | loop fusion | flops 524288 | bytes 3145728 | tf_op jit(solution)/shard_map/convert_element_type | solution.py:41
  10.2 0.7 gather_fusion.4
  10.9 0.7 copy.43
  11.6 7.3 %all-to-all-start.4 = ((f32[32,1,1]{2,1,0:T(1,128)}), f32[32,1,1]{2,1,0:T(1,128)S(1)}, u32[]{:S(2)}, u32[]{:S(2)}) async-start(f32[32,1,1]{2,1,0:T(1,128)} %copy.43), calls=%async_computation.5 | async-start | bytes 32768 | tf_op jit(solution)/shard_map/all_to_all | solution.py:34
  19.6 0.7 gather_fusion.2
  20.3 0.7 copy.40
  21.0 5.0 %all-to-all-done.4 = f32[32,1,1]{2,1,0:T(1,128)S(1)} async-done(((f32[32,1,1]{2,1,0:T(1,128)}), f32[32,1,1]{2,1,0:T(1,128)S(1)}, u32[]{:S(2)}, u32[]{:S(2)}) %all-to-all-start.4) | async-done | bytes 160 | tf_op jit(solution)/shard_map/all_to_all | solution.py:34
  26.0 2.5 %all-to-all-start.2 = ((f32[32,1,1]{2,1,0:T(1,128)}), f32[32,1,1]{2,1,0:T(1,128)S(1)}, u32[]{:S(2)}, u32[]{:S(2)}) async-start(f32[32,1,1]{2,1,0:T(1,128)} %copy.40), calls=%async_computation.2 | async-start | bytes 32768 | tf_op jit(solution)/shard_map/all_to_all | solution.py:30
  29.8 0.7 reshape.649
  30.5 5.2 %all-to-all-done.2 = f32[32,1,1]{2,1,0:T(1,128)S(1)} async-done(((f32[32,1,1]{2,1,0:T(1,128)}), f32[32,1,1]{2,1,0:T(1,128)S(1)}, u32[]{:S(2)}, u32[]{:S(2)}) %all-to-all-start.2) | async-done | bytes 160 | tf_op jit(solution)/shard_map/all_to_all | solution.py:30
  35.7 2.6 %all-to-all-start.3 = ((bf16[32,2,1024]{2,1,0:T(2,128)(2,1)}), bf16[32,2,1024]{2,1,0:T(2,128)(2,1)S(1)}, u32[]{:S(2)}, u32[]{:S(2)}) async-start(bf16[32,2,1024]{2,1,0:T(2,128)(2,1)} %reshape.649), calls=%async_computation.4 | async-start | bytes 262144 | tf_op jit(solution)/shard_map/all_to_all | solution.py:31
  39.0 0.7 reduce.3
  39.6 0.7 reshape.647
  40.4 6.3 %all-to-all-done.3 = bf16[32,2,1024]{2,1,0:T(2,128)(2,1)S(1)} async-done(((bf16[32,2,1024]{2,1,0:T(2,128)(2,1)}), bf16[32,2,1024]{2,1,0:T(2,128)(2,1)S(1)}, u32[]{:S(2)}, u32[]{:S(2)}) %all-to-all-start.3) | async-done | bytes 131104 | tf_op jit(solution)/shard_map/all_to_all | solution.py:31
  46.7 2.6 %all-to-all-start.1 = ((bf16[32,2,1024]{2,1,0:T(2,128)(2,1)}), bf16[32,2,1024]{2,1,0:T(2,128)(2,1)S(1)}, u32[]{:S(2)}, u32[]{:S(2)}) async-start(bf16[32,2,1024]{2,1,0:T(2,128)(2,1)} %reshape.647), calls=%async_computation.1 | async-start | bytes 262144 | tf_op jit(solution)/shard_map/all_to_all | solution.py:27
  49.9 1.0 copy.37
  50.9 6.7 %all-to-all-done.1 = bf16[32,2,1024]{2,1,0:T(2,128)(2,1)S(1)} async-done(((bf16[32,2,1024]{2,1,0:T(2,128)(2,1)}), bf16[32,2,1024]{2,1,0:T(2,128)(2,1)S(1)}, u32[]{:S(2)}, u32[]{:S(2)}) %all-to-all-start.1) | async-done | bytes 131104 | tf_op jit(solution)/shard_map/all_to_all | solution.py:27
  57.6 2.6 %all-to-all-start = ((f32[32,1,2048]{2,1,0:T(1,128)}), f32[32,1,2048]{2,1,0:T(1,128)S(1)}, u32[]{:S(2)}, u32[]{:S(2)}) async-start(f32[32,1,2048]{2,1,0:T(1,128)} %copy.37), calls=%async_computation | async-start | bytes 524288 | tf_op jit(solution)/shard_map/all_to_all | solution.py:26
  61.2 9.2 %all-to-all-done = f32[32,1,2048]{2,1,0:T(1,128)S(1)} async-done(((f32[32,1,2048]{2,1,0:T(1,128)}), f32[32,1,2048]{2,1,0:T(1,128)S(1)}, u32[]{:S(2)}, u32[]{:S(2)}) %all-to-all-start) | async-done | bytes 262176 | tf_op jit(solution)/shard_map/all_to_all | solution.py:26
  70.5 2.8 %fusion.24 = bf16[1,1,32,2048]{3,0,2,1:T(2,128)(2,1)S(1)} fusion(f32[1,1,1,32,2048]{4,3,1,0,2:T(8,128)} %reduce-scatter.2.cloned.1.call-done, f32[1,1,32,2048]{3,2,1,0:T(8,128)S(1)} %get-tuple-element.26, f32[32,1,2048]{2,1,0:T(1,128)S(1)} %all-to-all-done, f32[32]{0:T(128)S(1)} %reduce.1, bf16[32,1,2048]{2,1,0:T(2,128)(2,1)S(1)} %reshape.650), kind=kLoop, calls=%fused_computation.50 | loop fusion | flops 1114112 | bytes 1048704 | tf_op jit(solution)/shard_map/convert_element_type | solution.py:55
  73.3 0.7 copy.45
  75.2 1.2 %divide_convert_fusion = (bf16[1,32,2048]{2,1,0:T(8,128)(2,1)}, f32[1,32,2048]{2,1,0:T(8,128)}, bf16[1,32,2048]{2,1,0:T(8,128)(2,1)}) fusion(f32[32]{0:T(128)S(1)} %get-tuple-element.35, f32[1,1,1,32,2048]{4,3,1,0,2:T(8,128)S(1)} %copy-done.5, f32[32,1,2048]{2,1,0:T(1,128)S(1)} %convert_element_type.203, f32[32]{0:T(128)S(1)} %reduce.1, f32[32]{0:T(128)S(1)} %reduce, ...), kind=kLoop, calls=%fused_computation.47 | loop fusion | flops 1441792 | bytes 1442304 | tf_op jit(solution)/shard_map/convert_element_type | solution.py:54
  76.4 19.2 %all-gather.2.cloned.1.call-done = bf16[1,8,32,2048]{3,2,0,1:T(8,128)(2,1)} async-done(((bf16[1,1,32,2048]{3,2,0,1:T(8,128)(2,1)}), bf16[1,8,32,2048]{3,2,0,1:T(8,128)(2,1)}) %all-gather.2.cloned.1.call-update) | async-done | bytes 1048592 | tf_op jit(solution)/shard_map/all_gather | solution.py:56
  95.6 2.3 %copy.72 = bf16[1,8,32,2048]{3,2,1,0:T(8,128)(2,1)} copy(bf16[1,8,32,2048]{3,2,1,0:T(8,128)(2,1)} %bitcast.131) | data formatting | bytes 2097152
  (34 shorter events, 5.4 us)
Async XLA Ops:
  7.2 42.1 %copy-start = (f32[1,32,2048]{2,1,0:T(8,128)S(1)}, f32[1,32,2048]{2,1,0:T(8,128)}, u32[]{:S(2)}) copy-start(f32[1,32,2048]{2,1,0:T(8,128)} %param.8) | copy-start | bytes 786436
  7.2 3.0 %copy-start.6 = (s32[1,32]{1,0:T(1,128)S(1)}, s32[1,32]{1,0:T(1,128)}, u32[]{:S(2)}) copy-start(s32[1,32]{1,0:T(1,128)} %param.7) | copy-start | bytes 388
  7.2 3.0 %copy-start.1 = (f32[1,32]{1,0:T(1,128)S(1)}, f32[1,32]{1,0:T(1,128)}, u32[]{:S(2)}) copy-start(f32[1,32]{1,0:T(1,128)} %param.12) | copy-start | bytes 388
  7.2 63.3 %reduce-scatter.2.cloned.1.call-start = ((), (), s32[]{:S(2)}) async-start(), calls=%async_computation.6 | async-start | bytes 2359296 | tf_op jit(solution)/shard_map/reduce_scatter | solution.py:41
  10.1 8.8 %copy-start.3 = (bf16[1,32,2048]{2,1,0:T(8,128)(2,1)S(1)}, bf16[1,32,2048]{2,1,0:T(8,128)(2,1)}, u32[]{:S(2)}) copy-start(bf16[1,32,2048]{2,1,0:T(8,128)(2,1)} %param.11) | copy-start | bytes 393220
  10.1 9.5 %copy-start.2 = (f32[1,32]{1,0:T(1,128)S(1)}, f32[1,32]{1,0:T(1,128)}, u32[]{:S(2)}) copy-start(f32[1,32]{1,0:T(1,128)} %param.10) | copy-start | bytes 388
  10.1 28.2 %copy-start.4 = (bf16[1,32,2048]{2,1,0:T(8,128)(2,1)S(1)}, bf16[1,32,2048]{2,1,0:T(8,128)(2,1)}, u32[]{:S(2)}) copy-start(bf16[1,32,2048]{2,1,0:T(8,128)(2,1)} %param.9) | copy-start | bytes 393220
  11.6 14.5 %all-to-all-start.4 = ((f32[32,1,1]{2,1,0:T(1,128)}), f32[32,1,1]{2,1,0:T(1,128)S(1)}, u32[]{:S(2)}, u32[]{:S(2)}) async-start(f32[32,1,1]{2,1,0:T(1,128)} %copy.43), calls=%async_computation.5 | async-start | bytes 32768 | tf_op jit(solution)/shard_map/all_to_all | solution.py:34
  26.0 9.7 %all-to-all-start.2 = ((f32[32,1,1]{2,1,0:T(1,128)}), f32[32,1,1]{2,1,0:T(1,128)S(1)}, u32[]{:S(2)}, u32[]{:S(2)}) async-start(f32[32,1,1]{2,1,0:T(1,128)} %copy.40), calls=%async_computation.2 | async-start | bytes 32768 | tf_op jit(solution)/shard_map/all_to_all | solution.py:30
  35.7 11.0 %all-to-all-start.3 = ((bf16[32,2,1024]{2,1,0:T(2,128)(2,1)}), bf16[32,2,1024]{2,1,0:T(2,128)(2,1)S(1)}, u32[]{:S(2)}, u32[]{:S(2)}) async-start(bf16[32,2,1024]{2,1,0:T(2,128)(2,1)} %reshape.649), calls=%async_computation.4 | async-start | bytes 262144 | tf_op jit(solution)/shard_map/all_to_all | solution.py:31
  46.7 11.0 %all-to-all-start.1 = ((bf16[32,2,1024]{2,1,0:T(2,128)(2,1)}), bf16[32,2,1024]{2,1,0:T(2,128)(2,1)S(1)}, u32[]{:S(2)}, u32[]{:S(2)}) async-start(bf16[32,2,1024]{2,1,0:T(2,128)(2,1)} %reshape.647), calls=%async_computation.1 | async-start | bytes 262144 | tf_op jit(solution)/shard_map/all_to_all | solution.py:27
  57.6 12.8 %all-to-all-start = ((f32[32,1,2048]{2,1,0:T(1,128)}), f32[32,1,2048]{2,1,0:T(1,128)S(1)}, u32[]{:S(2)}, u32[]{:S(2)}) async-start(f32[32,1,2048]{2,1,0:T(1,128)} %copy.37), calls=%async_computation | async-start | bytes 524288 | tf_op jit(solution)/shard_map/all_to_all | solution.py:26
  60.2 35.3 %all-gather.2.cloned.1.call-start = ((), (), s32[]{:S(2)}) async-start(), calls=%async_computation.7 | async-start | bytes 1179648 | tf_op jit(solution)/shard_map/all_gather | solution.py:56
  70.5 3.8 %copy-start.5 = (f32[1,1,1,32,2048]{4,3,1,0,2:T(8,128)S(1)}, f32[1,1,1,32,2048]{4,3,1,0,2:T(8,128)}, u32[]{:S(2)}) copy-start(f32[1,1,1,32,2048]{4,3,1,0,2:T(8,128)} %reduce-scatter.2.cloned.1.call-done) | copy-start | bytes 786436
Sparse Core Ops, SparseCore 0:
  11.3 46.3 reduce-scatter.1
  74.1 21.3 all-gather.1
where the time goes:
time: 105 us
  waiting for transfers between devices  51.7 us (49%)
  starting transfers between devices  17.7 us (17%)
  between operations  14.2 us (14%)
  local copies, waits for them, and re-layouts  11 us (10%)
  other arithmetic  10.1 us (10%)
    all_gather x1, waiting for transfers between devices, on_device(): weights = lax.all_gather(local_weights, 'dp', axis=1, tiled=True)  19.2 us
    all_to_all x1, waiting for transfers between devices, on_device(): lax.all_to_all(shaped[0], ('dp', 'tensor'), split_axis=0, concat_axis=0,...  9.21 us
    all_to_all x1, starting transfers between devices, on_device(): lax.all_to_all(shaped[4], ('dp', 'tensor'), split_axis=0, concat_axis=0,...  7.33 us
    all_to_all x1, waiting for transfers between devices, on_device(): lax.all_to_all(shaped[1].astype(jnp.float32), ('dp', 'tensor'), split_axi...  6.73 us
    all_to_all x1, waiting for transfers between devices, on_device(): lax.all_to_all(shaped[3].astype(jnp.float32), ('dp', 'tensor'), split_axi...  6.3 us
    all_to_all x1, waiting for transfers between devices, on_device(): lax.all_to_all(shaped[2], ('dp', 'tensor'), split_axis=0, concat_axis=0,...  5.2 us
    all_to_all x1, waiting for transfers between devices, on_device(): lax.all_to_all(shaped[4], ('dp', 'tensor'), split_axis=0, concat_axis=0,...  5.05 us
    unnamed x19, local copies, waits for them, and re-layouts  4 us
  transfers between devices with their start and end apart: 7, of which 6 were waited for; matrix products, arithmetic and copies ran while one was open for 12% of the time, Pallas kernels for 0%

commit v1 on v0

v1 whole, which is shorter than its diff:
```python
import functools

import jax
import jax.numpy as jnp
from jax import lax
from jax.experimental import pallas as pl
from jax.experimental.pallas import tpu as pltpu
from jax.sharding import PartitionSpec as P

STEP = 10
LANES = 128
PARTS = 2
MESH = pl.DeviceIdType.MESH


def _kernel(nd, nt, slots, width, order_hbm, m_hbm, c1_hbm, s1_hbm, c2_hbm, s2_hbm, g_hbm,
            nm_out, nc1_out, ns1_out, nc2_out, ns2_out, wg,
            order_v, s1_v, s2_v, m_v, c1_v, c2_v,
            xs_m, xs_f, xs_c, xs_s, xr_m, xr_c, xr_s, gr, m1_v, m2_v,
            in_sem, rm, rc, rs, rg, sm, sc, ss, sg, ra, sa, rf, sf, lg):
    n = nd * nt
    per = slots // n
    chunks = width // LANES
    cp = chunks // PARTS
    wp = width // PARTS
    half_m = slots * cp
    half_c = slots * 2 * cp
    peers = nd // 2 - 1
    my_dp = lax.axis_index("dp")
    my_t = lax.axis_index("tensor")
    me = my_dp * nt + my_t
    partner = my_dp + 1 - 2 * lax.rem(my_dp, 2)

    loads = [
        pltpu.make_async_copy(order_hbm, order_v, in_sem.at[0]),
        pltpu.make_async_copy(s1_hbm, s1_v, in_sem.at[1]),
        pltpu.make_async_copy(s2_hbm, s2_v, in_sem.at[2]),
        pltpu.make_async_copy(m_hbm.at[0], m_v, in_sem.at[3]),
        pltpu.make_async_copy(c1_hbm.at[0], c1_v, in_sem.at[4]),
        pltpu.make_async_copy(c2_hbm.at[0], c2_v, in_sem.at[5]),
    ]
    for item in loads:
        item.start()

    barrier = pltpu.get_barrier_semaphore()

    def greet(k, carry):
        dst = lax.rem(me + k, n)
        pl.semaphore_signal(barrier, inc=1, device_id=(dst // nt, lax.rem(dst, nt)), device_id_type=MESH)
        return carry

    lax.fori_loop(1, n, greet, 0)

    def cols(h):
        return pl.ds(h * wp, wp)

    own_grad = [
        pltpu.make_async_copy(g_hbm.at[0, 0, my_dp, :, cols(h)], gr.at[my_dp, :, cols(h)], rg.at[h])
        for h in range(PARTS)
    ]
    for item in own_grad:
        item.start()

    for item in loads:
        item.wait()
    row = lax.broadcasted_iota(jnp.int32, (slots, slots), 0)
    lane = lax.broadcasted_iota(jnp.int32, (slots, slots), 1)
    eye = row == lane
    order_f = order_v[...].astype(jnp.float32)
    order_col = jnp.sum(jnp.where(eye, order_f, 0.0), axis=1, keepdims=True)
    pick = order_col == lane.astype(jnp.float32)
    s1_col = jnp.sum(jnp.where(pick, s1_v[...], 0.0), axis=1, keepdims=True)
    s2_col = jnp.sum(jnp.where(pick, s2_v[...], 0.0), axis=1, keepdims=True)
    side = lax.broadcasted_iota(jnp.int32, (slots, LANES), 1) < LANES // 2
    xs_s[pl.ds(0, slots, stride=8), :] = jnp.where(side, s1_col, s2_col)
    select = jnp.where(pick, 1.0, 0.0).astype(jnp.bfloat16)

    def take(x):
        return jnp.dot(select, x, preferred_element_type=jnp.float32)

    def stage(h):
        x = m_v[:, cols(h)]
        hi = x.astype(jnp.bfloat16)
        rest = x - hi.astype(jnp.float32)
        mid = rest.astype(jnp.bfloat16)
        low = (rest - mid.astype(jnp.float32)).astype(jnp.bfloat16)
        xm = (take(hi) + take(mid)) + take(low)
        x1 = take(c1_v[:, cols(h)])
        x2 = take(c2_v[:, cols(h)])
        for j in range(cp):
            piece = slice(j * LANES, (j + 1) * LANES)
            xs_m[pl.ds(h * half_m + j, slots, stride=cp), :] = xm[:, piece]
            xs_f[pl.ds(h * half_c + j, slots, stride=2 * cp), :] = x1[:, piece]
            xs_f[pl.ds(h * half_c + cp + j, slots, stride=2 * cp), :] = x2[:, piece]
        xs_c[pl.ds(h * half_c, half_c), :] = xs_f[pl.ds(h * half_c, half_c), :].astype(jnp.bfloat16)

    stage(0)

    pl.semaphore_wait(barrier, n - 1)

    def send_grads(h):
        def one(k, carry):
            dst = lax.rem(my_dp + k, nd)
            pltpu.make_async_remote_copy(
                src_ref=g_hbm.at[0, 0, dst, :, cols(h)], dst_ref=gr.at[my_dp, :, cols(h)],
                send_sem=sg.at[h], recv_sem=rg.at[h], device_id=(dst, my_t), device_id_type=MESH,
            ).start()
            return carry

        lax.fori_loop(1, nd, one, 0)

    bm = per * cp
    bc = per * 2 * cp
    bs = per * 8

    def send_blocks(h):
        def one(k, carry):
            dst = lax.rem(me + k, n)
            where = (dst // nt, lax.rem(dst, nt))
            pltpu.make_async_remote_copy(
                src_ref=xs_m.at[pl.ds(pl.multiple_of(h * half_m + dst * bm, 8), bm)],
                dst_ref=xr_m.at[pl.ds(pl.multiple_of(h * half_m + me * bm, 8), bm)],
                send_sem=sm.at[h], recv_sem=rm.at[h], device_id=where, device_id_type=MESH,
            ).start()
            pltpu.make_async_remote_copy(
                src_ref=xs_c.at[pl.ds(pl.multiple_of(h * half_c + dst * bc, 16), bc)],
                dst_ref=xr_c.at[pl.ds(pl.multiple_of(h * half_c + me * bc, 16), bc)],
                send_sem=sc.at[h], recv_sem=rc.at[h], device_id=where, device_id_type=MESH,
            ).start()
            if h == 0:
                pltpu.make_async_remote_copy(
                    src_ref=xs_s.at[pl.ds(pl.multiple_of(dst * bs, 8), bs)],
                    dst_ref=xr_s.at[pl.ds(pl.multiple_of(me * bs, 8), bs)],
                    send_sem=ss.at[0], recv_sem=rs.at[0], device_id=where, device_id_type=MESH,
                ).start()
            return carry

        lax.fori_loop(1, n, one, 0)
        at_m = pl.ds(pl.multiple_of(h * half_m + me * bm, 8), bm)
        at_c = pl.ds(pl.multiple_of(h * half_c + me * bc, 16), bc)
        pltpu.make_async_copy(xs_m.at[at_m], xr_m.at[at_m], rm.at[h]).start()
        pltpu.make_async_copy(xs_c.at[at_c], xr_c.at[at_c], rc.at[h]).start()
        if h == 0:
            at_s = pl.ds(pl.multiple_of(me * bs, 8), bs)
            pltpu.make_async_copy(xs_s.at[at_s], xr_s.at[at_s], rs.at[0]).start()

    def drain(ref, sem):
        pltpu.make_async_copy(ref, ref, sem).wait()

    send_grads(0)
    send_blocks(0)
    for h in range(1, PARTS):
        stage(h)
        send_blocks(h)
        send_grads(h)

    inv_one = 1.0 / (1.0 - 0.9**STEP)
    inv_two = 1.0 / (1.0 - 0.95**STEP)

    def adam(h, s1, s2, tops):
        drain(xr_m.at[pl.ds(h * half_m, half_m)], rm.at[h])
        drain(xr_c.at[pl.ds(h * half_c, half_c)], rc.at[h])
        drain(gr.at[:, :, cols(h)], rg.at[h])
        xs_f[pl.ds(h * half_c, half_c), :] = xr_c[pl.ds(h * half_c, half_c), :].astype(jnp.float32)
        top1, top2 = tops
        for j in range(cp):
            at = slice((h * cp + j) * LANES, (h * cp + j + 1) * LANES)
            grad = gr[0, :, at].astype(jnp.float32)
            for p in range(1, nd):
                grad = grad + gr[p, :, at].astype(jnp.float32)
            first = xs_f[pl.ds(h * half_c + j, slots, stride=2 * cp), :] * s1
            second = xs_f[pl.ds(h * half_c + cp + j, slots, stride=2 * cp), :] * s2
            old = xr_m[pl.ds(h * half_m + j, slots, stride=cp), :]
            one = 0.9 * first + 0.1 * grad
            two = 0.95 * second + 0.05 * grad * grad
            update = (one * inv_one) / (jnp.sqrt(two * inv_two) + 1e-08) + 0.1 * old
            new = old - 0.01 * update
            nm_out[0, :, at] = new
            wg[0, my_dp, :, at] = new.astype(jnp.bfloat16)
            m1_v[:, at] = one
            m2_v[:, at] = two
            top1 = jnp.maximum(top1, jnp.abs(one))
            top2 = jnp.maximum(top2, jnp.abs(two))
        return top1, top2

    def gathered(src, h):
        return wg.at[0, src, :, cols(h)]

    def to_peer(h, j):
        dst = lax.rem(my_dp + 2 * j, nd)
        return pltpu.make_async_remote_copy(
            src_ref=gathered(my_dp, h), dst_ref=gathered(my_dp, h),
            send_sem=sa.at[h, j], recv_sem=ra.at[h, j], device_id=(dst, my_t), device_id_type=MESH,
        )

    def to_partner(h, j):
        src = lax.rem(my_dp + nd - 2 * j, nd)
        return pltpu.make_async_remote_copy(
            src_ref=gathered(src, h), dst_ref=gathered(src, h),
            send_sem=sf.at[h, j], recv_sem=rf.at[h, j], device_id=(partner, my_t), device_id_type=MESH,
        )

    def forward(h):
        for j in range(1, peers + 1):
            to_peer(h, j).wait_recv()
            to_partner(h, j).start()

    drain(xr_s, rs.at[0])
    got = xr_s[pl.ds(0, slots, stride=8), :]
    s1 = got[:, 0:1]
    s2 = got[:, LANES // 2:LANES // 2 + 1]
    zero = jnp.zeros((slots, LANES), jnp.float32)
    tops = (zero, zero)
    for h in range(PARTS):
        tops = adam(h, s1, s2, tops)
        for j in range(1, peers + 1):
            to_peer(h, j).start()
        to_partner(h, 0).start()
        if h > 0:
            forward(h - 1)

    top1 = jnp.max(tops[0], axis=1, keepdims=True) + 1e-06
    top2 = jnp.max(tops[1], axis=1, keepdims=True) + 1e-06
    ns1_out[...] = jnp.sum(jnp.where(eye, top1, 0.0), axis=0, keepdims=True)
    ns2_out[...] = jnp.sum(jnp.where(eye, top2, 0.0), axis=0, keepdims=True)
    inv1 = 1.0 / top1
    inv2 = 1.0 / top2
    for j in range(chunks):
        at = slice(j * LANES, (j + 1) * LANES)
        nc1_out[0, :, at] = (m1_v[:, at] * inv1).astype(jnp.bfloat16)
        nc2_out[0, :, at] = (m2_v[:, at] * inv2).astype(jnp.bfloat16)

    forward(PARTS - 1)
    for h in range(PARTS):
        for j in range(peers + 1):
            to_partner(h, j).wait()
        for j in range(1, peers + 1):
            to_peer(h, j).wait_send()
        drain(xs_m.at[pl.ds(0, half_m - bm)], sm.at[h])
        drain(xs_c.at[pl.ds(0, half_c - bc)], sc.at[h])
        drain(gr.at[pl.ds(0, nd - 1), :, cols(h)], sg.at[h])
    drain(xs_s.at[pl.ds(0, slots * 8 - bs)], ss.at[0])


def on_device(send_order, master, first_code, first_scale, second_code, second_scale, grads):
    nd = lax.axis_size("dp")
    nt = lax.axis_size("tensor")
    slots = master.shape[1]
    width = master.shape[2]
    f32, b16 = jnp.float32, jnp.bfloat16
    rows = slots * width // LANES
    dma = pltpu.SemaphoreType.DMA
    ring = nd // 2
    return pl.pallas_call(
        functools.partial(_kernel, nd, nt, slots, width),
        out_shape=(
            jax.ShapeDtypeStruct((1, slots, width), f32),
            jax.ShapeDtypeStruct((1, slots, width), b16),
            jax.ShapeDtypeStruct((1, slots), f32),
            jax.ShapeDtypeStruct((1, slots, width), b16),
            jax.ShapeDtypeStruct((1, slots), f32),
            jax.ShapeDtypeStruct((1, nd, slots, width), b16),
        ),
        in_specs=[pl.BlockSpec(memory_space=pl.ANY)] * 7,
        out_specs=[pl.BlockSpec(memory_space=pltpu.VMEM)] * 6,
        scratch_shapes=[
            pltpu.VMEM((1, slots), jnp.int32),
            pltpu.VMEM((1, slots), f32),
            pltpu.VMEM((1, slots), f32),
            pltpu.VMEM((slots, width), f32),
            pltpu.VMEM((slots, width), b16),
            pltpu.VMEM((slots, width), b16),
            pltpu.VMEM((rows, LANES), f32),
            pltpu.VMEM((2 * rows, LANES), f32),
            pltpu.VMEM((2 * rows, LANES), b16),
            pltpu.VMEM((slots * 8, LANES), f32),
            pltpu.VMEM((rows, LANES), f32),
            pltpu.VMEM((2 * rows, LANES), b16),
            pltpu.VMEM((slots * 8, LANES), f32),
            pltpu.VMEM((nd, slots, width), b16),
            pltpu.VMEM((slots, width), f32),
            pltpu.VMEM((slots, width), f32),
            dma((6,)),
            dma((PARTS,)), dma((PARTS,)), dma((1,)), dma((PARTS,)),
            dma((PARTS,)), dma((PARTS,)), dma((1,)), dma((PARTS,)),
            dma((PARTS, ring)), dma((PARTS, ring)), dma((PARTS, ring)), dma((PARTS, ring)),
            dma((1,)),
        ],
        compiler_params=pltpu.CompilerParams(collective_id=0, has_side_effects=True),
        name="relayout_adam",
    )(send_order, master, first_code, first_scale, second_code, second_scale, grads)


def solution(mesh):
    placed = (
        P(("dp", "tensor"), None),
        P(("dp", "tensor"), None, None),
        P(("dp", "tensor"), None, None),
        P(("dp", "tensor"), None),
        P(("dp", "tensor"), None, None),
        P(("dp", "tensor"), None),
        P("dp", "tensor", None, None, None),
    )
    return jax.shard_map(
        on_device,
        mesh=mesh,
        in_specs=placed,
        out_specs=(
            P(("dp", "tensor"), None, None),
            P(("dp", "tensor"), None, None),
            P(("dp", "tensor"), None),
            P(("dp", "tensor"), None, None),
            P(("dp", "tensor"), None),
            P("tensor", None, None, None),
        ),
        check_vma=False,
    )
```

time: 105 us -> 44.3 us (0.42)
  waiting for transfers between devices: 51.7 us -> 0 us
  Pallas kernels: 0 us -> 35.9 us
  starting transfers between devices: 17.7 us -> 0 us
  between operations: 14.2 us -> 0.65 us
  other arithmetic: 10.1 us -> 0 us
  local copies, waits for them, and re-layouts: 11 us -> 7.56 us
    pallas_call x0 -> x1, Pallas kernels: none -> 35.9 us  [on_device(): pl.pallas_call(functools.partial(_kernel, nd, nt, slots, width), out_shap...]
    all_to_all x5 -> x0, waiting for transfers between devices: 32.5 us -> none  [the longest x1 9.21 us: on_device(): lax.all_to_all(shaped[0], ('dp', 'tensor'), split_axis=0, concat_axis=0,...]
    all_gather x1 -> x0, waiting for transfers between devices: 19.2 us -> none  [on_device(): weights = lax.all_gather(local_weights, 'dp', axis=1, tiled=True)]
    all_to_all x5 -> x0, starting transfers between devices: 17.6 us -> none  [the longest x1 7.33 us: on_device(): lax.all_to_all(shaped[4], ('dp', 'tensor'), split_axis=0, concat_axis=0,...]
    convert_element_type x6 -> x0, other arithmetic: 8.5 us -> none  [the longest x1 2.86 us: on_device(): grads.astype(jnp.float32)]
    unnamed x19 -> x10, local copies, waits for them, and re-layouts: 4 us -> 7.56 us
    gather x5 -> x0, local copies, waits for them, and re-layouts: 3.35 us -> none  [the longest x1 0.7 us: on_device(): second_scale[0][order_row]]
    all_to_all x2 -> x0, local copies, waits for them, and re-layouts: 1.4 us -> none  [the longest x1 0.7 us: on_device(): lax.all_to_all(shaped[2], ('dp', 'tensor'), split_axis=0, concat_axis=0,...]
  transfers between devices with their start and end apart: 7 -> 0, of which waited for: 6 -> 0; matrix products, arithmetic and copies ran while one was open for 12% -> 0% of each run, Pallas kernels for 0% -> 0%
where the time goes in v1:
time: 44.3 us; the launch traced here: 44.1 us
  Pallas kernels  35.9 us (81%)
  local copies, waits for them, and re-layouts  7.56 us (17%)
  between operations  0.65 us (1%)
    pallas_call x1, Pallas kernels, on_device(): pl.pallas_call(functools.partial(_kernel, nd, nt, slots, width), out_shap...  35.9 us
    unnamed x10, local copies, waits for them, and re-layouts  7.56 us

profile of v1, /device:TPU:0, one launch (start us, length us, event | category | flops | bytes accessed | tf_op | source)
XLA Modules:
  0.0 44.1 jit_solution(5500007377769073396)
XLA Ops:
  0.6 35.9 %relayout_adam.1 = (f32[1,32,2048]{2,1,0:T(8,128)}, bf16[1,32,2048]{2,1,0:T(8,128)(2,1)}, f32[1,32]{1,0:T(1,128)}, bf16[1,32,2048]{2,1,0:T(8,128)(2,1)}, f32[1,3...) custom-call(s32[1,32]{1,0:T(1,128)} %order_hbm.1, f32[1,32,2048]{2,1,0:T(8,128)} %m_hbm.1, bf16[1,32,2048]{2,1,0:T(8,128)(2,1)} %c1_hbm.1, ...), custom_call_target="tpu_custom_call" | custom-call | tf_op jit(solution)/shard_map/relayout_adam/pallas_call | solution.py:254
  36.5 0.0 copy-start
  36.5 1.8 %copy.19 = f32[1,32,2048]{2,1,0:T(8,128)} copy(f32[1,32,2048]{2,1,0:T(8,128)} %get-tuple-element.12) | data formatting | bytes 524288
  38.3 1.6 %copy.20 = bf16[1,32,2048]{2,1,0:T(8,128)(2,1)} copy(bf16[1,32,2048]{2,1,0:T(8,128)(2,1)} %get-tuple-element.13) | data formatting | bytes 262144
  39.9 1.2 %copy.21 = f32[1,32]{1,0:T(1,128)} copy(f32[1,32]{1,0:T(1,128)} %get-tuple-element.14) | data formatting | bytes 256
  41.0 0.0 copy-start.1
  41.0 1.6 %copy.22 = bf16[1,32,2048]{2,1,0:T(8,128)(2,1)} copy(bf16[1,32,2048]{2,1,0:T(8,128)(2,1)} %get-tuple-element.15) | data formatting | bytes 262144
  42.6 0.0 copy-done.1
  42.6 0.5 %copy.23 = f32[1,32]{1,0:T(1,128)} copy(f32[1,32]{1,0:T(1,128)S(1)} %copy-done.1) | data formatting | bytes 256
  43.1 0.0 copy-done
  43.1 1.0 %copy.24 = bf16[1,8,32,2048]{3,2,1,0:T(8,128)(2,1)} copy(bf16[1,8,32,2048]{3,2,1,0:T(8,128)(2,1)S(1)} %copy-done) | data formatting | bytes 2097152
Async XLA Ops:
  36.5 6.6 %copy-start = (bf16[1,8,32,2048]{3,2,1,0:T(8,128)(2,1)S(1)}, bf16[1,8,32,2048]{3,2,1,0:T(8,128)(2,1)}, u32[]{:S(2)}) copy-start(bf16[1,8,32,2048]{3,2,1,0:T(8,128)(2,1)} %get-tuple-element.17) | copy-start | bytes 3145732
  41.0 1.6 %copy-start.1 = (f32[1,32]{1,0:T(1,128)S(1)}, f32[1,32]{1,0:T(1,128)}, u32[]{:S(2)}) copy-start(f32[1,32]{1,0:T(1,128)} %get-tuple-element.16) | copy-start | bytes 388

commit v2 on v1

--- a/solution.py
+++ b/solution.py
@@ -17,7 +17,7 @@
             nm_out, nc1_out, ns1_out, nc2_out, ns2_out, wg,
             order_v, s1_v, s2_v, m_v, c1_v, c2_v,
             xs_m, xs_f, xs_c, xs_s, xr_m, xr_c, xr_s, gr, m1_v, m2_v,
-            in_sem, rm, rc, rs, rg, sm, sc, ss, sg, ra, sa, rf, sf, lg):
+            in_sem, rm, rc, rs, rg, sm, sc, ss, sg, ra, sa, rf, sf):
     n = nd * nt
     per = slots // n
     chunks = width // LANES
@@ -72,7 +72,7 @@
     s1_col = jnp.sum(jnp.where(pick, s1_v[...], 0.0), axis=1, keepdims=True)
     s2_col = jnp.sum(jnp.where(pick, s2_v[...], 0.0), axis=1, keepdims=True)
     side = lax.broadcasted_iota(jnp.int32, (slots, LANES), 1) < LANES // 2
-    xs_s[pl.ds(0, slots, stride=8), :] = jnp.where(side, s1_col, s2_col)
+    xs_s[:, 0, :] = jnp.where(side, s1_col, s2_col)
     select = jnp.where(pick, 1.0, 0.0).astype(jnp.bfloat16)
 
     def take(x):
@@ -111,7 +111,7 @@
 
     bm = per * cp
     bc = per * 2 * cp
-    bs = per * 8
+    bs = per
 
     def send_blocks(h):
         def one(k, carry):
@@ -129,8 +129,8 @@
             ).start()
             if h == 0:
                 pltpu.make_async_remote_copy(
-                    src_ref=xs_s.at[pl.ds(pl.multiple_of(dst * bs, 8), bs)],
-                    dst_ref=xr_s.at[pl.ds(pl.multiple_of(me * bs, 8), bs)],
+                    src_ref=xs_s.at[pl.ds(dst * bs, bs)],
+                    dst_ref=xr_s.at[pl.ds(me * bs, bs)],
                     send_sem=ss.at[0], recv_sem=rs.at[0], device_id=where, device_id_type=MESH,
                 ).start()
             return carry
@@ -141,7 +141,7 @@
         pltpu.make_async_copy(xs_m.at[at_m], xr_m.at[at_m], rm.at[h]).start()
         pltpu.make_async_copy(xs_c.at[at_c], xr_c.at[at_c], rc.at[h]).start()
         if h == 0:
-            at_s = pl.ds(pl.multiple_of(me * bs, 8), bs)
+            at_s = pl.ds(me * bs, bs)
             pltpu.make_async_copy(xs_s.at[at_s], xr_s.at[at_s], rs.at[0]).start()
 
     def drain(ref, sem):
@@ -206,7 +206,7 @@
             to_partner(h, j).start()
 
     drain(xr_s, rs.at[0])
-    got = xr_s[pl.ds(0, slots, stride=8), :]
+    got = xr_s[:, 0, :]
     s1 = got[:, 0:1]
     s2 = got[:, LANES // 2:LANES // 2 + 1]
     zero = jnp.zeros((slots, LANES), jnp.float32)
@@ -239,10 +239,21 @@
         drain(xs_m.at[pl.ds(0, half_m - bm)], sm.at[h])
         drain(xs_c.at[pl.ds(0, half_c - bc)], sc.at[h])
         drain(gr.at[pl.ds(0, nd - 1), :, cols(h)], sg.at[h])
-    drain(xs_s.at[pl.ds(0, slots * 8 - bs)], ss.at[0])
+    drain(xs_s.at[pl.ds(0, slots - bs)], ss.at[0])
+
+
+def _write_out(*refs):
+    sem = refs[-1]
+    count = (len(refs) - 1) // 2
+    copies = [pltpu.make_async_copy(refs[i], refs[count + i], sem.at[i]) for i in range(count)]
+    for item in copies:
+        item.start()
+    for item in copies:
+        item.wait()
 
 
 def on_device(send_order, master, first_code, first_scale, second_code, second_scale, grads):
+    arrays = (send_order, master, first_code, first_scale, second_code, second_scale, grads)
     nd = lax.axis_size("dp")
     nt = lax.axis_size("tensor")
     slots = master.shape[1]
@@ -251,17 +262,19 @@
     rows = slots * width // LANES
     dma = pltpu.SemaphoreType.DMA
     ring = nd // 2
-    return pl.pallas_call(
+    grant = slots * width * (40 + 2 * nd) + slots * 4096 + 6 * 1024 * 1024
+    results = (
+        ((1, slots, width), f32),
+        ((1, slots, width), b16),
+        ((1, slots), f32),
+        ((1, slots, width), b16),
+        ((1, slots), f32),
+        ((1, nd, slots, width), b16),
+    )
+    held = pl.pallas_call(
         functools.partial(_kernel, nd, nt, slots, width),
-        out_shape=(
-            jax.ShapeDtypeStruct((1, slots, width), f32),
-            jax.ShapeDtypeStruct((1, slots, width), b16),
-            jax.ShapeDtypeStruct((1, slots), f32),
-            jax.ShapeDtypeStruct((1, slots, width), b16),
-            jax.ShapeDtypeStruct((1, slots), f32),
-            jax.ShapeDtypeStruct((1, nd, slots, width), b16),
-        ),
-        in_specs=[pl.BlockSpec(memory_space=pl.ANY)] * 7,
+        out_shape=tuple(pltpu.VMEM(*item) for item in results),
+        in_specs=[pl.BlockSpec(memory_space=pltpu.HBM)] * 7,
         out_specs=[pl.BlockSpec(memory_space=pltpu.VMEM)] * 6,
         scratch_shapes=[
             pltpu.VMEM((1, slots), jnp.int32),
@@ -273,10 +286,10 @@
             pltpu.VMEM((rows, LANES), f32),
             pltpu.VMEM((2 * rows, LANES), f32),
             pltpu.VMEM((2 * rows, LANES), b16),
-            pltpu.VMEM((slots * 8, LANES), f32),
+            pltpu.VMEM((slots, 1, LANES), f32),
             pltpu.VMEM((rows, LANES), f32),
             pltpu.VMEM((2 * rows, LANES), b16),
-            pltpu.VMEM((slots * 8, LANES), f32),
+            pltpu.VMEM((slots, 1, LANES), f32),
             pltpu.VMEM((nd, slots, width), b16),
             pltpu.VMEM((slots, width), f32),
             pltpu.VMEM((slots, width), f32),
@@ -284,11 +297,19 @@
             dma((PARTS,)), dma((PARTS,)), dma((1,)), dma((PARTS,)),
             dma((PARTS,)), dma((PARTS,)), dma((1,)), dma((PARTS,)),
             dma((PARTS, ring)), dma((PARTS, ring)), dma((PARTS, ring)), dma((PARTS, ring)),
-            dma((1,)),
         ],
-        compiler_params=pltpu.CompilerParams(collective_id=0, has_side_effects=True),
+        compiler_params=pltpu.CompilerParams(collective_id=0, has_side_effects=True, vmem_limit_bytes=grant),
         name="relayout_adam",
-    )(send_order, master, first_code, first_scale, second_code, second_scale, grads)
+    )(*(pltpu.with_memory_space_constraint(item, pltpu.HBM) for item in arrays))
+    return pl.pallas_call(
+        _write_out,
+        out_shape=tuple(jax.ShapeDtypeStruct(*item) for item in results),
+        in_specs=[pl.BlockSpec(memory_space=pltpu.VMEM)] * len(results),
+        out_specs=[pl.BlockSpec(memory_space=pltpu.HBM)] * len(results),
+        scratch_shapes=[dma((len(results),))],
+        compiler_params=pltpu.CompilerParams(vmem_limit_bytes=2 * 1024 * 1024),
+        name="write_out",
+    )(*(pltpu.with_memory_space_constraint(item, pltpu.VMEM) for item in held))
 
 
 def solution(mesh):

time: 44.3 us -> 35.4 us (0.80)
  local copies, waits for them, and re-layouts: 7.56 us -> 0 us
  Pallas kernels: 35.9 us -> 34.6 us
    unnamed x10 -> x0, local copies, waits for them, and re-layouts: 7.56 us -> none
    pallas_call x1, Pallas kernels: 35.9 us -> 33.4 us  [on_device(): pl.pallas_call(functools.partial(_kernel, nd, nt, slots, width), out_shap...]
    pallas_call x0 -> x1, Pallas kernels: none -> 1.21 us  [on_device(): pl.pallas_call(_write_out, out_shape=tuple((jax.ShapeDtypeStruct(*item) f...]
where the time goes in v2:
time: 35.4 us; the launch traced here: 35.2 us
  Pallas kernels  34.6 us (98%)
  between operations  0.64 us (2%)
    pallas_call x1, Pallas kernels, on_device(): pl.pallas_call(functools.partial(_kernel, nd, nt, slots, width), out_shap...  33.4 us
    pallas_call x1, Pallas kernels, on_device(): pl.pallas_call(_write_out, out_shape=tuple((jax.ShapeDtypeStruct(*item) f...  1.21 us

profile of v2, /device:TPU:0, one launch (start us, length us, event | category | flops | bytes accessed | tf_op | source)
XLA Modules:
  0.0 35.2 jit_solution(10701290643071765435)
XLA Ops:
  0.6 33.4 %relayout_adam.1 = (f32[1,32,2048]{2,1,0:T(8,128)S(1)}, bf16[1,32,2048]{2,1,0:T(8,128)(2,1)S(1)}, f32[1,32]{1,0:T(1,128)S(1)}, bf16[1,32,2048]{2,1,0:T(8,128)(2,...) custom-call(s32[1,32]{1,0:T(1,128)} %order_hbm.1, f32[1,32,2048]{2,1,0:T(8,128)} %m_hbm.1, ...), custom_call_target="tpu_custom_call" | custom-call | tf_op jit(solution)/shard_map/relayout_adam/pallas_call | solution.py:274
  34.0 1.2 %write_out.1 = (f32[1,32,2048]{2,1,0:T(8,128)}, bf16[1,32,2048]{2,1,0:T(8,128)(2,1)}, f32[1,32]{1,0:T(1,128)}, bf16[1,32,2048]{2,1,0:T(8,128)(2,1)}, f32[1,32]{1,0:T(1,128)}, /*index=5*/bf16[1,8,32,2048]{3,2,1,0:T(8,128)(2,1)}) custom-call(f32[1,32,2048]{2,1,0:T(8,128)S(1)} %get-tuple-element.12.refs_0_, bf16[1,32,2048]{2,1,0:T(8,128)(2,1)S(1)} %get-tuple-element.13.refs_1_, ...), custom_call_target="tpu_custom_call" | custom-call | tf_op jit(solution)/shard_map/write_out/pallas_call | solution.py:304

commit v3 on v2

--- a/solution.py
+++ b/solution.py
@@ -9,27 +9,39 @@
 
 STEP = 10
 LANES = 128
-PARTS = 2
+RELAYS = 2
+PARTS = 4
 MESH = pl.DeviceIdType.MESH
 
 
 def _kernel(nd, nt, slots, width, order_hbm, m_hbm, c1_hbm, s1_hbm, c2_hbm, s2_hbm, g_hbm,
             nm_out, nc1_out, ns1_out, nc2_out, ns2_out, wg,
             order_v, s1_v, s2_v, m_v, c1_v, c2_v,
-            xs_m, xs_f, xs_c, xs_s, xr_m, xr_c, xr_s, gr, m1_v, m2_v,
-            in_sem, rm, rc, rs, rg, sm, sc, ss, sg, ra, sa, rf, sf):
+            xs_m, xs_f, xs_c, xs_s, xr_m, xr_c, xr_s, raw_x, raw_y, out_x, out_y, got_x, got_y, m1_v, m2_v,
+            in_sem, rm, rc, rs, rg, sm, sc, ss, sg, rh, sh, ra, sa, rf, sf):
     n = nd * nt
     per = slots // n
     chunks = width // LANES
-    cp = chunks // PARTS
+    cp = chunks // RELAYS
+    cq = chunks // PARTS
+    wr = width // RELAYS
     wp = width // PARTS
     half_m = slots * cp
     half_c = slots * 2 * cp
-    peers = nd // 2 - 1
+    ny = nd // 4
+    chips = 2 * ny
     my_dp = lax.axis_index("dp")
     my_t = lax.axis_index("tensor")
     me = my_dp * nt + my_t
-    partner = my_dp + 1 - 2 * lax.rem(my_dp, 2)
+    my_c = lax.rem(my_dp, 2)
+    my_chip = my_dp // 2
+    my_x = lax.rem(my_chip, 2)
+    my_y = my_chip // 2
+    partner = my_dp + 1 - 2 * my_c
+
+    def dp_of(y, x, c):
+        return (y * 2 + x) * 2 + c
+
 
     loads = [
         pltpu.make_async_copy(order_hbm, order_v, in_sem.at[0]),
@@ -54,12 +66,19 @@
     def cols(h):
         return pl.ds(h * wp, wp)
 
-    own_grad = [
-        pltpu.make_async_copy(g_hbm.at[0, 0, my_dp, :, cols(h)], gr.at[my_dp, :, cols(h)], rg.at[h])
-        for h in range(PARTS)
-    ]
-    for item in own_grad:
-        item.start()
+    def wide(r):
+        return pl.ds(r * wr, wr)
+
+    def slabs(h, y, x, c):
+        if h % 2 == 0:
+            return g_hbm.at[:, x, c, :, cols(h)]
+        return g_hbm.at[y, :, c, :, cols(h)]
+
+    def raw_at(h, y, x, c):
+        return raw_x.at[h // 2, x, c] if h % 2 == 0 else raw_y.at[h // 2, y, c]
+
+    for h in range(PARTS):
+        pltpu.make_async_copy(slabs(h, my_y, my_x, my_c), raw_at(h, my_y, my_x, my_c), rg.at[h]).start()
 
     for item in loads:
         item.wait()
@@ -79,14 +98,14 @@
         return jnp.dot(select, x, preferred_element_type=jnp.float32)
 
     def stage(h):
-        x = m_v[:, cols(h)]
+        x = m_v[:, wide(h)]
         hi = x.astype(jnp.bfloat16)
         rest = x - hi.astype(jnp.float32)
         mid = rest.astype(jnp.bfloat16)
         low = (rest - mid.astype(jnp.float32)).astype(jnp.bfloat16)
         xm = (take(hi) + take(mid)) + take(low)
-        x1 = take(c1_v[:, cols(h)])
-        x2 = take(c2_v[:, cols(h)])
+        x1 = take(c1_v[:, wide(h)])
+        x2 = take(c2_v[:, wide(h)])
         for j in range(cp):
             piece = slice(j * LANES, (j + 1) * LANES)
             xs_m[pl.ds(h * half_m + j, slots, stride=cp), :] = xm[:, piece]
@@ -98,16 +117,53 @@
 
     pl.semaphore_wait(barrier, n - 1)
 
+    def drain(ref, sem):
+        pltpu.make_async_copy(ref, ref, sem).wait()
+
     def send_grads(h):
+        group = 2 if h % 2 == 0 else ny
+
         def one(k, carry):
-            dst = lax.rem(my_dp + k, nd)
+            step = lax.rem(k, 2 * group)
+            c = lax.rem(my_c + step, 2)
+            away = step // 2
+            if h % 2 == 0:
+                y, x = my_y, lax.rem(my_x + away, 2)
+            else:
+                y, x = lax.rem(my_y + away, ny), my_x
             pltpu.make_async_remote_copy(
-                src_ref=g_hbm.at[0, 0, dst, :, cols(h)], dst_ref=gr.at[my_dp, :, cols(h)],
-                send_sem=sg.at[h], recv_sem=rg.at[h], device_id=(dst, my_t), device_id_type=MESH,
+                src_ref=slabs(h, y, x, c), dst_ref=raw_at(h, my_y, my_x, my_c),
+                send_sem=sg.at[h], recv_sem=rg.at[h], device_id=(dp_of(y, x, c), my_t), device_id_type=MESH,
             ).start()
             return carry
 
-        lax.fori_loop(1, nd, one, 0)
+        lax.fori_loop(2, 2 * group, one, 0)
+        one(1, 0)
+
+    def second(h):
+        return (out_x, got_x, ny, my_y) if h % 2 == 0 else (out_y, got_y, 2, my_x)
+
+    def hand_on(h):
+        k = h // 2
+        raw = (raw_x if h % 2 == 0 else raw_y).at[k]
+        drain(raw, rg.at[h])
+        out, got, size, mine = second(h)
+        for t in range(size):
+            for i in range(cq):
+                at = slice(i * LANES, (i + 1) * LANES)
+                terms = [raw[u, c, t, :, at].astype(jnp.float32) for u in range(raw.shape[0]) for c in range(2)]
+                out[k, t, :, at] = functools.reduce(jnp.add, terms)
+
+        def one(away, carry):
+            t = lax.rem(mine + away, size)
+            where = dp_of(t, my_x, my_c) if h % 2 == 0 else dp_of(my_y, t, my_c)
+            pltpu.make_async_remote_copy(
+                src_ref=out.at[k, t], dst_ref=got.at[k, mine],
+                send_sem=sh.at[h], recv_sem=rh.at[h], device_id=(where, my_t), device_id_type=MESH,
+            ).start()
+            return carry
+
+        lax.fori_loop(1, size, one, 0)
 
     bm = per * cp
     bc = per * 2 * cp
@@ -144,35 +200,41 @@
             at_s = pl.ds(me * bs, bs)
             pltpu.make_async_copy(xs_s.at[at_s], xr_s.at[at_s], rs.at[0]).start()
 
-    def drain(ref, sem):
-        pltpu.make_async_copy(ref, ref, sem).wait()
-
-    send_grads(0)
+    for h in range(PARTS):
+        send_grads(h)
     send_blocks(0)
-    for h in range(1, PARTS):
-        stage(h)
-        send_blocks(h)
-        send_grads(h)
+    for r in range(1, RELAYS):
+        stage(r)
+        send_blocks(r)
+
+    for h in range(PARTS):
+        hand_on(h)
 
     inv_one = 1.0 / (1.0 - 0.9**STEP)
     inv_two = 1.0 / (1.0 - 0.95**STEP)
 
     def adam(h, s1, s2, tops):
-        drain(xr_m.at[pl.ds(h * half_m, half_m)], rm.at[h])
-        drain(xr_c.at[pl.ds(h * half_c, half_c)], rc.at[h])
-        drain(gr.at[:, :, cols(h)], rg.at[h])
-        xs_f[pl.ds(h * half_c, half_c), :] = xr_c[pl.ds(h * half_c, half_c), :].astype(jnp.float32)
+        if h * RELAYS % PARTS == 0:
+            r = h * RELAYS // PARTS
+            drain(xr_m.at[pl.ds(r * half_m, half_m)], rm.at[r])
+            drain(xr_c.at[pl.ds(r * half_c, half_c)], rc.at[r])
+            xs_f[pl.ds(r * half_c, half_c), :] = xr_c[pl.ds(r * half_c, half_c), :].astype(jnp.float32)
+        out, got, size, mine = second(h)
+        k = h // 2
+        drain(got.at[k, pl.ds(0, size - 1)], rh.at[h])
         top1, top2 = tops
-        for j in range(cp):
-            at = slice((h * cp + j) * LANES, (h * cp + j + 1) * LANES)
-            grad = gr[0, :, at].astype(jnp.float32)
-            for p in range(1, nd):
-                grad = grad + gr[p, :, at].astype(jnp.float32)
-            first = xs_f[pl.ds(h * half_c + j, slots, stride=2 * cp), :] * s1
-            second = xs_f[pl.ds(h * half_c + cp + j, slots, stride=2 * cp), :] * s2
-            old = xr_m[pl.ds(h * half_m + j, slots, stride=cp), :]
+        for i in range(h * cq, (h + 1) * cq):
+            at = slice(i * LANES, (i + 1) * LANES)
+            r, j = i // cp, i % cp
+            near = slice((i - h * cq) * LANES, (i - h * cq + 1) * LANES)
+            grad = out[k, mine, :, near]
+            for away in range(1, size):
+                grad = grad + got[k, lax.rem(mine + away, size), :, near]
+            first = xs_f[pl.ds(r * half_c + j, slots, stride=2 * cp), :] * s1
+            other = xs_f[pl.ds(r * half_c + cp + j, slots, stride=2 * cp), :] * s2
+            old = xr_m[pl.ds(r * half_m + j, slots, stride=cp), :]
             one = 0.9 * first + 0.1 * grad
-            two = 0.95 * second + 0.05 * grad * grad
+            two = 0.95 * other + 0.05 * grad * grad
             update = (one * inv_one) / (jnp.sqrt(two * inv_two) + 1e-08) + 0.1 * old
             new = old - 0.01 * update
             nm_out[0, :, at] = new
@@ -183,41 +245,58 @@
             top2 = jnp.maximum(top2, jnp.abs(two))
         return top1, top2
 
-    def gathered(src, h):
-        return wg.at[0, src, :, cols(h)]
-
-    def to_peer(h, j):
-        dst = lax.rem(my_dp + 2 * j, nd)
+    def gathered(chip, c, h):
+        return wg.at[0, chip * 2 + c, :, cols(h)]
+
+    def to_chip(h, chip, y, x):
+        slab = gathered(chip, my_c, h)
         return pltpu.make_async_remote_copy(
-            src_ref=gathered(my_dp, h), dst_ref=gathered(my_dp, h),
-            send_sem=sa.at[h, j], recv_sem=ra.at[h, j], device_id=(dst, my_t), device_id_type=MESH,
+            src_ref=slab, dst_ref=slab, send_sem=sa.at[h], recv_sem=ra.at[h, chip],
+            device_id=(dp_of(y, x, my_c), my_t), device_id_type=MESH,
         )
 
-    def to_partner(h, j):
-        src = lax.rem(my_dp + nd - 2 * j, nd)
+    def to_partner(h, chip):
+        slab = gathered(chip, my_c, h)
         return pltpu.make_async_remote_copy(
-            src_ref=gathered(src, h), dst_ref=gathered(src, h),
-            send_sem=sf.at[h, j], recv_sem=rf.at[h, j], device_id=(partner, my_t), device_id_type=MESH,
+            src_ref=slab, dst_ref=slab, send_sem=sf.at[h], recv_sem=rf.at[h],
+            device_id=(partner, my_t), device_id_type=MESH,
         )
 
-    def forward(h):
-        for j in range(1, peers + 1):
-            to_peer(h, j).wait_recv()
-            to_partner(h, j).start()
+    def arrived(h, chip):
+        slab = gathered(chip, my_c, h)
+        pltpu.make_async_copy(slab, slab, ra.at[h, chip]).wait()
+        to_partner(h, chip).start()
+
+    across = 1 - my_x
+    rows_away = [lax.rem(my_y + away, ny) for away in range(1, ny)]
+
+    def spread(h):
+        to_chip(h, my_chip, my_y, across).start()
+        for y in rows_away:
+            to_chip(h, my_chip, y, my_x).start()
+            to_chip(h, my_chip, y, across).start()
+        to_partner(h, my_chip).start()
+
+    def relay(h):
+        arrived(h, my_y * 2 + across)
+        for y in rows_away:
+            arrived(h, y * 2 + my_x)
+
+    def finish(h):
+        for y in rows_away:
+            arrived(h, y * 2 + across)
 
     drain(xr_s, rs.at[0])
-    got = xr_s[:, 0, :]
-    s1 = got[:, 0:1]
-    s2 = got[:, LANES // 2:LANES // 2 + 1]
+    scales = xr_s[:, 0, :]
+    s1 = scales[:, 0:1]
+    s2 = scales[:, LANES // 2:LANES // 2 + 1]
     zero = jnp.zeros((slots, LANES), jnp.float32)
     tops = (zero, zero)
     for h in range(PARTS):
         tops = adam(h, s1, s2, tops)
-        for j in range(1, peers + 1):
-            to_peer(h, j).start()
-        to_partner(h, 0).start()
-        if h > 0:
-            forward(h - 1)
+        spread(h)
+    for h in range(PARTS - 1):
+        relay(h)
 
     top1 = jnp.max(tops[0], axis=1, keepdims=True) + 1e-06
     top2 = jnp.max(tops[1], axis=1, keepdims=True) + 1e-06
@@ -230,15 +309,22 @@
         nc1_out[0, :, at] = (m1_v[:, at] * inv1).astype(jnp.bfloat16)
         nc2_out[0, :, at] = (m2_v[:, at] * inv2).astype(jnp.bfloat16)
 
-    forward(PARTS - 1)
-    for h in range(PARTS):
-        for j in range(peers + 1):
-            to_partner(h, j).wait()
-        for j in range(1, peers + 1):
-            to_peer(h, j).wait_send()
-        drain(xs_m.at[pl.ds(0, half_m - bm)], sm.at[h])
-        drain(xs_c.at[pl.ds(0, half_c - bc)], sc.at[h])
-        drain(gr.at[pl.ds(0, nd - 1), :, cols(h)], sg.at[h])
+    relay(PARTS - 1)
+    for h in range(PARTS):
+        finish(h)
+    for h in range(PARTS):
+        out, got, size, mine = second(h)
+        k = h // 2
+        theirs = wg.at[0, pl.ds(0, chips), :, cols(h)]
+        drain(theirs, rf.at[h])
+        drain(theirs, sf.at[h])
+        drain(wg.at[0, pl.ds(0, chips - 1), :, cols(h)], sa.at[h])
+        drain(got.at[k, pl.ds(0, size - 1)], sh.at[h])
+        group = 2 if h % 2 == 0 else ny
+        drain(wg.at[0, pl.ds(0, (2 * group - 1) * (nd // (2 * group))), :, cols(h)], sg.at[h])
+    for r in range(RELAYS):
+        drain(xs_m.at[pl.ds(0, half_m - bm)], sm.at[r])
+        drain(xs_c.at[pl.ds(0, half_c - bc)], sc.at[r])
     drain(xs_s.at[pl.ds(0, slots - bs)], ss.at[0])
 
 
@@ -261,8 +347,11 @@
     f32, b16 = jnp.float32, jnp.bfloat16
     rows = slots * width // LANES
     dma = pltpu.SemaphoreType.DMA
-    ring = nd // 2
-    grant = slots * width * (40 + 2 * nd) + slots * 4096 + 6 * 1024 * 1024
+    ny = nd // 4
+    pairs = PARTS // 2
+    wp = width // PARTS
+    arrays = arrays[:6] + (grads.reshape(ny, 2, 2, slots, width),)
+    grant = slots * width * (40 + 6 * nd) + slots * 4096 + 6 * 1024 * 1024
     results = (
         ((1, slots, width), f32),
         ((1, slots, width), b16),
@@ -290,13 +379,19 @@
             pltpu.VMEM((rows, LANES), f32),
             pltpu.VMEM((2 * rows, LANES), b16),
             pltpu.VMEM((slots, 1, LANES), f32),
-            pltpu.VMEM((nd, slots, width), b16),
+            pltpu.VMEM((pairs, 2, 2, ny, slots, wp), b16),
+            pltpu.VMEM((pairs, ny, 2, 2, slots, wp), b16),
+            pltpu.VMEM((pairs, ny, slots, wp), f32),
+            pltpu.VMEM((pairs, 2, slots, wp), f32),
+            pltpu.VMEM((pairs, ny, slots, wp), f32),
+            pltpu.VMEM((pairs, 2, slots, wp), f32),
             pltpu.VMEM((slots, width), f32),
             pltpu.VMEM((slots, width), f32),
             dma((6,)),
-            dma((PARTS,)), dma((PARTS,)), dma((1,)), dma((PARTS,)),
-            dma((PARTS,)), dma((PARTS,)), dma((1,)), dma((PARTS,)),
-            dma((PARTS, ring)), dma((PARTS, ring)), dma((PARTS, ring)), dma((PARTS, ring)),
+            dma((RELAYS,)), dma((RELAYS,)), dma((1,)), dma((PARTS,)),
+            dma((RELAYS,)), dma((RELAYS,)), dma((1,)), dma((PARTS,)),
+            dma((PARTS,)), dma((PARTS,)),
+            dma((PARTS, 2 * ny)), dma((PARTS,)), dma((PARTS,)), dma((PARTS,)),
         ],
         compiler_params=pltpu.CompilerParams(collective_id=0, has_side_effects=True, vmem_limit_bytes=grant),
         name="relayout_adam",

time: 35.4 us -> 33.3 us (0.941)
  Pallas kernels: 34.6 us -> 32.5 us
    pallas_call x1, Pallas kernels: 33.4 us -> 31.3 us  [on_device(): pl.pallas_call(functools.partial(_kernel, nd, nt, slots, width), out_shap...]
where the time goes in v3:
time: 33.3 us; the launch traced here: 33.1 us
  Pallas kernels  32.5 us (98%)
  between operations  0.64 us (2%)
    pallas_call x1, Pallas kernels, on_device(): pl.pallas_call(functools.partial(_kernel, nd, nt, slots, width), out_shap...  31.3 us
    pallas_call x1, Pallas kernels, on_device(): pl.pallas_call(_write_out, out_shape=tuple((jax.ShapeDtypeStruct(*item) f...  1.21 us

profile of v3, /device:TPU:0, one launch (start us, length us, event | category | flops | bytes accessed | tf_op | source)
XLA Modules:
  0.0 33.1 jit_solution(9660719944342128534)
XLA Ops:
  0.6 31.3 %relayout_adam.1 = (f32[1,32,2048]{2,1,0:T(8,128)S(1)}, bf16[1,32,2048]{2,1,0:T(8,128)(2,1)S(1)}, f32[1,32]{1,0:T(1,128)S(1)}, bf16[1,32,2048]{2,1,0:T(8,128)(2,...) custom-call(s32[1,32]{1,0:T(1,128)} %order_hbm.1, f32[1,32,2048]{2,1,0:T(8,128)} %m_hbm.1, ...), custom_call_target="tpu_custom_call" | custom-call | tf_op jit(solution)/shard_map/relayout_adam/pallas_call | solution.py:363
  31.9 1.2 %write_out.1 = (f32[1,32,2048]{2,1,0:T(8,128)}, bf16[1,32,2048]{2,1,0:T(8,128)(2,1)}, f32[1,32]{1,0:T(1,128)}, bf16[1,32,2048]{2,1,0:T(8,128)(2,1)}, f32[1,32]{1,0:T(1,128)}, /*index=5*/bf16[1,8,32,2048]{3,2,1,0:T(8,128)(2,1)}) custom-call(f32[1,32,2048]{2,1,0:T(8,128)S(1)} %get-tuple-element.12.refs_0_, bf16[1,32,2048]{2,1,0:T(8,128)(2,1)S(1)} %get-tuple-element.13.refs_1_, ...), custom_call_target="tpu_custom_call" | custom-call | tf_op jit(solution)/shard_map/write_out/pallas_call | solution.py:399
